TPU v7x, 128 devices: a whole 4x4x4 slice. The times are simulated.
128 devices in a mesh: blk: 8 (over z_lo, y), inner: 16 (over x, z_hi, core).
Axes of the slice: x: 4, y: 4, z: 4 (z_hi: 2, z_lo: 2; z = z_hi * 2 + z_lo), core: 2. Of those that a mesh axis runs over, the one named last changes fastest.
Arguments:
- queries: bfloat16 [16384, 768], P(('blk', 'inner')), may hold values from -16 to 16
- keys: bfloat16 [16384, 768], P(('blk', 'inner')), may hold values from -16 to 16
- values: bfloat16 [16384, 768], P(('blk', 'inner')), may hold values from -6 to 6
- valid: int32 [16384], P(('blk', 'inner')), may hold values 0 or 1
- out_weight: bfloat16 [768, 768], replicated, may hold values from -0.21875 to 0.21875
Outputs:
- mixed: bfloat16 [16384, 768], P(('blk', 'inner'))
All inputs are finite; a program needn't handle non-finite values. No bound on the sum of `valid` on one device may be relied on, other than what follows from the above.
Results may differ from a plain program's by a relative error of at most 0.015.
Values may be sent and summed in bfloat16 or wider, within the bound.
A program may use at most 128 MiB of HBM per device.

v0:
```python
import jax
import jax.numpy as jnp
from jax import lax
from jax.sharding import PartitionSpec as P

HEADS = 12
HEAD_DIM = 64


def make_fold(query_all):
    query_count = query_all.shape[0]
    query_heads = query_all.reshape(query_count, HEADS, HEAD_DIM)
    score_scale = HEAD_DIM ** (-0.5)

    def attend(state_now, piece, start):
        key_piece, value_piece, flag_piece = piece
        piece_rows = key_piece.shape[0]
        block_rows = 128
        count = piece_rows // block_rows
        key_blocks = key_piece.reshape(count, block_rows, HEADS, HEAD_DIM)
        value_blocks = value_piece.reshape(count, block_rows, HEADS, HEAD_DIM)
        flag_blocks = flag_piece.reshape(count, block_rows)

        def one_block(carry, item):
            run_max, row_total, weighted = carry
            key_heads, value_heads, flag_block = item
            scores = (
                jnp.einsum(
                    "qhd,khd->hqk", query_heads, key_heads, preferred_element_type=jnp.float32
                )
                * score_scale
            )
            scores = jnp.where(flag_block[None, None, :] > 0, scores, -1e30)
            new_max = jnp.maximum(run_max, jnp.max(scores, axis=-1))
            shrink = jnp.exp(run_max - new_max)
            chances = jnp.exp(scores - new_max[..., None]).astype(jnp.bfloat16)
            row_total = row_total * shrink + jnp.sum(chances, axis=-1, dtype=jnp.float32)
            weighted = weighted * shrink[..., None] + jnp.einsum(
                "hqk,khd->hqd", chances, value_heads, preferred_element_type=jnp.float32
            )
            return ((new_max, row_total, weighted), None)

        state_end, unused = lax.scan(one_block, state_now, (key_blocks, value_blocks, flag_blocks))
        return state_end

    starting = (
        jnp.zeros((HEADS, query_count), jnp.float32),
        jnp.zeros((HEADS, query_count), jnp.float32),
        jnp.zeros((HEADS, query_count, HEAD_DIM), jnp.float32),
    )
    return (attend, starting)


def settle(top, row_total, weighted):
    return weighted / (jnp.exp(-top) + row_total)[..., None]


def combine_loop(state_end, own_rows):
    run_max, row_total, weighted = state_end
    top = lax.pmax(run_max, "blk")
    shrink = jnp.exp(run_max - top)
    total_own, weighted_own = (
        lax.psum_scatter(row_total * shrink, "blk", scatter_dimension=1, tiled=True),
        lax.psum_scatter(weighted * shrink[..., None], "blk", scatter_dimension=1, tiled=True),
    )
    top_own = lax.dynamic_slice_in_dim(top, lax.axis_index("blk") * own_rows, own_rows, 1)
    return settle(top_own, total_own, weighted_own)


def on_device(queries, keys, values, valid, out_weight):
    own_rows = queries.shape[0]
    width = queries.shape[1]
    flags = valid.astype(jnp.bfloat16)
    query_all = lax.all_gather(queries, "blk", axis=0, tiled=True)
    attend, starting = make_fold(query_all)
    state_end = attend(
        starting,
        (
            lax.all_gather(keys, "inner", axis=0, tiled=True),
            lax.all_gather(values, "inner", axis=0, tiled=True),
            lax.all_gather(flags, "inner", axis=0, tiled=True),
        ),
        jnp.int32(0),
    )
    attended = combine_loop(state_end, own_rows)
    attended = jnp.transpose(attended, (1, 0, 2)).reshape(own_rows, width).astype(jnp.bfloat16)
    return jnp.dot(attended, out_weight, preferred_element_type=jnp.float32).astype(jnp.bfloat16)


def solution(mesh):
    return jax.shard_map(
        on_device,
        mesh=mesh,
        in_specs=(
            P(("blk", "inner"), None),
            P(("blk", "inner"), None),
            P(("blk", "inner"), None),
            P(("blk", "inner")),
            P(),
        ),
        out_specs=P(("blk", "inner"), None),
        check_vma=False,
    )
```

profile of v0, /device:TPU:0, one launch (start us, length us, event | category | flops | bytes accessed | tf_op | source)
XLA Modules:
  0.0 532.3 jit_solution(9887534371943158650)
XLA Ops:
  9.5 25.0 %all-gather = bf16[16,1,128]{2,1,0:T(2,128)(2,1)S(1)} all-gather(bf16[1,1,128]{2,1,0:T(2,128)(2,1)S(1)} %convert_bitcast_fusion), channel_id=1, replica_groups=mesh['blk'=8,'inner'=16] {'inner'}, dimensions={0}, use_global_device_ids=true | all-gather | bytes 4352 | tf_op jit(solution)/shard_map/all_gather | solution.py:81
  34.4 17.7 %all-gather.7.cloned.1.call-done = bf16[1024,768]{1,0:T(8,128)(2,1)} async-done(((bf16[128,768]{1,0:T(8,128)(2,1)}), bf16[1024,768]{1,0:T(8,128)(2,1)}) %all-gather.7.cloned.1.call-update) | async-done | bytes 1572880 | tf_op jit(solution)/shard_map/all_gather | solution.py:74
  53.8 52.2 %all-gather.5.cloned.1.call-done = bf16[2048,768]{1,0:T(8,128)(2,1)} async-done(((bf16[128,768]{1,0:T(8,128)(2,1)}), bf16[2048,768]{1,0:T(8,128)(2,1)}) %all-gather.5.cloned.1.call-update) | async-done | bytes 3145744 | tf_op jit(solution)/shard_map/all_gather | solution.py:79
  116.3 43.1 %all-gather.9.cloned.1.call-done = bf16[2048,768]{1,0:T(8,128)(2,1)} async-done(((bf16[128,768]{1,0:T(8,128)(2,1)}), bf16[2048,768]{1,0:T(8,128)(2,1)}) %all-gather.9.cloned.1.call-update) | async-done | bytes 3145744 | tf_op jit(solution)/shard_map/all_gather | solution.py:80
  169.5 238.6 %while.15 = (s32[]{:T(128)}, f32[12,1024]{1,0:T(8,128)S(1)}, f32[12,1024]{1,0:T(8,128)S(1)}, f32[12,1024,64]{1,2,0:T(8,128)}, bf16[16,128]{1,0:T(8,128)(2,1)S(1)...) while((s32[]{:T(128)}, f32[12,1024]{1,0:T(8,128)S(1)}, ...), condition=%wide.region_3.4_spmd.clone, body=%wide.region_0.3_spmd.clone.sunk | while | flops 425521536 | bytes 53086096 | solution.py:43
  169.5 4.8 bitcast_reduce_fusion.2
  192.8 5.5 %fusion.25 = f32[12,1024,64]{1,2,0:T(8,128)} fusion(f32[12,1024,64]{1,2,0:T(8,128)} %get-tuple-element.187, f32[12,1024]{1,0:T(8,128)S(1)} %get-tuple-element.173, pred[]{:T(512)S(6)} %compare.3, bf16[16,128,12,64]{1,3,2,0:T(8,128)(2,1)} %get-tuple-element.201, s32[]{:T(128)} %get-tuple-element.184, f32[12,128,1024]{2,1,0:T(8,128)S(1)} %copy-done.1, ...), kind=kOutput, calls=%fused_computation.7.clone.1 | convolution fusion | flops 209977344 | bytes 12878465 | tf_op jit(solution)/shard_map/while/body/eval_jaxpr/hqk,khd->hqd/dot_general | solution.py:38
  207.8 5.5 %fusion.25 = f32[12,1024,64]{1,2,0:T(8,128)} fusion(f32[12,1024,64]{1,2,0:T(8,128)} %get-tuple-element.187, f32[12,1024]{1,0:T(8,128)S(1)} %get-tuple-element.173, pred[]{:T(512)S(6)} %compare.3, bf16[16,128,12,64]{1,3,2,0:T(8,128)(2,1)} %get-tuple-element.201, s32[]{:T(128)} %get-tuple-element.184, f32[12,128,1024]{2,1,0:T(8,128)S(1)} %copy-done.1, ...), kind=kOutput, calls=%fused_computation.7.clone.1 | convolution fusion | flops 209977344 | bytes 12878465 | tf_op jit(solution)/shard_map/while/body/eval_jaxpr/hqk,khd->hqd/dot_general | solution.py:38
  222.8 5.5 %fusion.25 = f32[12,1024,64]{1,2,0:T(8,128)} fusion(f32[12,1024,64]{1,2,0:T(8,128)} %get-tuple-element.187, f32[12,1024]{1,0:T(8,128)S(1)} %get-tuple-element.173, pred[]{:T(512)S(6)} %compare.3, bf16[16,128,12,64]{1,3,2,0:T(8,128)(2,1)} %get-tuple-element.201, s32[]{:T(128)} %get-tuple-element.184, f32[12,128,1024]{2,1,0:T(8,128)S(1)} %copy-done.1, ...), kind=kOutput, calls=%fused_computation.7.clone.1 | convolution fusion | flops 209977344 | bytes 12878465 | tf_op jit(solution)/shard_map/while/body/eval_jaxpr/hqk,khd->hqd/dot_general | solution.py:38
  237.8 5.5 %fusion.25 = f32[12,1024,64]{1,2,0:T(8,128)} fusion(f32[12,1024,64]{1,2,0:T(8,128)} %get-tuple-element.187, f32[12,1024]{1,0:T(8,128)S(1)} %get-tuple-element.173, pred[]{:T(512)S(6)} %compare.3, bf16[16,128,12,64]{1,3,2,0:T(8,128)(2,1)} %get-tuple-element.201, s32[]{:T(128)} %get-tuple-element.184, f32[12,128,1024]{2,1,0:T(8,128)S(1)} %copy-done.1, ...), kind=kOutput, calls=%fused_computation.7.clone.1 | convolution fusion | flops 209977344 | bytes 12878465 | tf_op jit(solution)/shard_map/while/body/eval_jaxpr/hqk,khd->hqd/dot_general | solution.py:38
  252.7 5.5 %fusion.25 = f32[12,1024,64]{1,2,0:T(8,128)} fusion(f32[12,1024,64]{1,2,0:T(8,128)} %get-tuple-element.187, f32[12,1024]{1,0:T(8,128)S(1)} %get-tuple-element.173, pred[]{:T(512)S(6)} %compare.3, bf16[16,128,12,64]{1,3,2,0:T(8,128)(2,1)} %get-tuple-element.201, s32[]{:T(128)} %get-tuple-element.184, f32[12,128,1024]{2,1,0:T(8,128)S(1)} %copy-done.1, ...), kind=kOutput, calls=%fused_computation.7.clone.1 | convolution fusion | flops 209977344 | bytes 12878465 | tf_op jit(solution)/shard_map/while/body/eval_jaxpr/hqk,khd->hqd/dot_general | solution.py:38
  267.7 5.5 %fusion.25 = f32[12,1024,64]{1,2,0:T(8,128)} fusion(f32[12,1024,64]{1,2,0:T(8,128)} %get-tuple-element.187, f32[12,1024]{1,0:T(8,128)S(1)} %get-tuple-element.173, pred[]{:T(512)S(6)} %compare.3, bf16[16,128,12,64]{1,3,2,0:T(8,128)(2,1)} %get-tuple-element.201, s32[]{:T(128)} %get-tuple-element.184, f32[12,128,1024]{2,1,0:T(8,128)S(1)} %copy-done.1, ...), kind=kOutput, calls=%fused_computation.7.clone.1 | convolution fusion | flops 209977344 | bytes 12878465 | tf_op jit(solution)/shard_map/while/body/eval_jaxpr/hqk,khd->hqd/dot_general | solution.py:38
  282.7 5.5 %fusion.25 = f32[12,1024,64]{1,2,0:T(8,128)} fusion(f32[12,1024,64]{1,2,0:T(8,128)} %get-tuple-element.187, f32[12,1024]{1,0:T(8,128)S(1)} %get-tuple-element.173, pred[]{:T(512)S(6)} %compare.3, bf16[16,128,12,64]{1,3,2,0:T(8,128)(2,1)} %get-tuple-element.201, s32[]{:T(128)} %get-tuple-element.184, f32[12,128,1024]{2,1,0:T(8,128)S(1)} %copy-done.1, ...), kind=kOutput, calls=%fused_computation.7.clone.1 | convolution fusion | flops 209977344 | bytes 12878465 | tf_op jit(solution)/shard_map/while/body/eval_jaxpr/hqk,khd->hqd/dot_general | solution.py:38
  297.7 5.5 %fusion.25 = f32[12,1024,64]{1,2,0:T(8,128)} fusion(f32[12,1024,64]{1,2,0:T(8,128)} %get-tuple-element.187, f32[12,1024]{1,0:T(8,128)S(1)} %get-tuple-element.173, pred[]{:T(512)S(6)} %compare.3, bf16[16,128,12,64]{1,3,2,0:T(8,128)(2,1)} %get-tuple-element.201, s32[]{:T(128)} %get-tuple-element.184, f32[12,128,1024]{2,1,0:T(8,128)S(1)} %copy-done.1, ...), kind=kOutput, calls=%fused_computation.7.clone.1 | convolution fusion | flops 209977344 | bytes 12878465 | tf_op jit(solution)/shard_map/while/body/eval_jaxpr/hqk,khd->hqd/dot_general | solution.py:38
  312.7 5.5 %fusion.25 = f32[12,1024,64]{1,2,0:T(8,128)} fusion(f32[12,1024,64]{1,2,0:T(8,128)} %get-tuple-element.187, f32[12,1024]{1,0:T(8,128)S(1)} %get-tuple-element.173, pred[]{:T(512)S(6)} %compare.3, bf16[16,128,12,64]{1,3,2,0:T(8,128)(2,1)} %get-tuple-element.201, s32[]{:T(128)} %get-tuple-element.184, f32[12,128,1024]{2,1,0:T(8,128)S(1)} %copy-done.1, ...), kind=kOutput, calls=%fused_computation.7.clone.1 | convolution fusion | flops 209977344 | bytes 12878465 | tf_op jit(solution)/shard_map/while/body/eval_jaxpr/hqk,khd->hqd/dot_general | solution.py:38
  327.6 5.5 %fusion.25 = f32[12,1024,64]{1,2,0:T(8,128)} fusion(f32[12,1024,64]{1,2,0:T(8,128)} %get-tuple-element.187, f32[12,1024]{1,0:T(8,128)S(1)} %get-tuple-element.173, pred[]{:T(512)S(6)} %compare.3, bf16[16,128,12,64]{1,3,2,0:T(8,128)(2,1)} %get-tuple-element.201, s32[]{:T(128)} %get-tuple-element.184, f32[12,128,1024]{2,1,0:T(8,128)S(1)} %copy-done.1, ...), kind=kOutput, calls=%fused_computation.7.clone.1 | convolution fusion | flops 209977344 | bytes 12878465 | tf_op jit(solution)/shard_map/while/body/eval_jaxpr/hqk,khd->hqd/dot_general | solution.py:38
  342.6 5.5 %fusion.25 = f32[12,1024,64]{1,2,0:T(8,128)} fusion(f32[12,1024,64]{1,2,0:T(8,128)} %get-tuple-element.187, f32[12,1024]{1,0:T(8,128)S(1)} %get-tuple-element.173, pred[]{:T(512)S(6)} %compare.3, bf16[16,128,12,64]{1,3,2,0:T(8,128)(2,1)} %get-tuple-element.201, s32[]{:T(128)} %get-tuple-element.184, f32[12,128,1024]{2,1,0:T(8,128)S(1)} %copy-done.1, ...), kind=kOutput, calls=%fused_computation.7.clone.1 | convolution fusion | flops 209977344 | bytes 12878465 | tf_op jit(solution)/shard_map/while/body/eval_jaxpr/hqk,khd->hqd/dot_general | solution.py:38
  357.6 5.5 %fusion.25 = f32[12,1024,64]{1,2,0:T(8,128)} fusion(f32[12,1024,64]{1,2,0:T(8,128)} %get-tuple-element.187, f32[12,1024]{1,0:T(8,128)S(1)} %get-tuple-element.173, pred[]{:T(512)S(6)} %compare.3, bf16[16,128,12,64]{1,3,2,0:T(8,128)(2,1)} %get-tuple-element.201, s32[]{:T(128)} %get-tuple-element.184, f32[12,128,1024]{2,1,0:T(8,128)S(1)} %copy-done.1, ...), kind=kOutput, calls=%fused_computation.7.clone.1 | convolution fusion | flops 209977344 | bytes 12878465 | tf_op jit(solution)/shard_map/while/body/eval_jaxpr/hqk,khd->hqd/dot_general | solution.py:38
  372.6 5.5 %fusion.25 = f32[12,1024,64]{1,2,0:T(8,128)} fusion(f32[12,1024,64]{1,2,0:T(8,128)} %get-tuple-element.187, f32[12,1024]{1,0:T(8,128)S(1)} %get-tuple-element.173, pred[]{:T(512)S(6)} %compare.3, bf16[16,128,12,64]{1,3,2,0:T(8,128)(2,1)} %get-tuple-element.201, s32[]{:T(128)} %get-tuple-element.184, f32[12,128,1024]{2,1,0:T(8,128)S(1)} %copy-done.1, ...), kind=kOutput, calls=%fused_computation.7.clone.1 | convolution fusion | flops 209977344 | bytes 12878465 | tf_op jit(solution)/shard_map/while/body/eval_jaxpr/hqk,khd->hqd/dot_general | solution.py:38
  387.6 5.5 %fusion.25 = f32[12,1024,64]{1,2,0:T(8,128)} fusion(f32[12,1024,64]{1,2,0:T(8,128)} %get-tuple-element.187, f32[12,1024]{1,0:T(8,128)S(1)} %get-tuple-element.173, pred[]{:T(512)S(6)} %compare.3, bf16[16,128,12,64]{1,3,2,0:T(8,128)(2,1)} %get-tuple-element.201, s32[]{:T(128)} %get-tuple-element.184, f32[12,128,1024]{2,1,0:T(8,128)S(1)} %copy-done.1, ...), kind=kOutput, calls=%fused_computation.7.clone.1 | convolution fusion | flops 209977344 | bytes 12878465 | tf_op jit(solution)/shard_map/while/body/eval_jaxpr/hqk,khd->hqd/dot_general | solution.py:38
  402.6 5.5 %fusion.25 = f32[12,1024,64]{1,2,0:T(8,128)} fusion(f32[12,1024,64]{1,2,0:T(8,128)} %get-tuple-element.187, f32[12,1024]{1,0:T(8,128)S(1)} %get-tuple-element.173, pred[]{:T(512)S(6)} %compare.3, bf16[16,128,12,64]{1,3,2,0:T(8,128)(2,1)} %get-tuple-element.201, s32[]{:T(128)} %get-tuple-element.184, f32[12,128,1024]{2,1,0:T(8,128)S(1)} %copy-done.1, ...), kind=kOutput, calls=%fused_computation.7.clone.1 | convolution fusion | flops 209977344 | bytes 12878465 | tf_op jit(solution)/shard_map/while/body/eval_jaxpr/hqk,khd->hqd/dot_general | solution.py:38
  408.1 33.8 %pmax.7 = f32[12,1024]{1,0:T(8,128)S(1)} all-reduce(f32[12,1024]{1,0:T(8,128)S(1)} %get-tuple-element.50), channel_id=1, replica_groups=mesh['blk'=8,'inner'=16] {'blk'}, use_global_device_ids=true, to_apply=%region_4.5 | all-reduce | flops 12288 | bytes 98304 | tf_op jit(solution)/shard_map/pmax | solution.py:60
  446.8 29.9 %reduce-scatter.5.cloned.1.call-done = f32[12,128]{1,0:T(8,128)} async-done(((f32[12,1024]{1,0:T(8,128)}), f32[12,128]{1,0:T(8,128)}) %reduce-scatter.5.cloned.1.call-update) | async-done | bytes 6160 | tf_op jit(solution)/shard_map/reduce_scatter | solution.py:63
  477.3 46.4 %reduce-scatter.3.cloned.1.call-done = f32[12,128,64]{1,2,0:T(8,128)} async-done(((f32[12,1024,64]{1,2,0:T(8,128)}), f32[12,128,64]{1,2,0:T(8,128)}) %reduce-scatter.3.cloned.1.call-update) | async-done | bytes 393232 | tf_op jit(solution)/shard_map/reduce_scatter | solution.py:64
  (157 shorter events, 183.0 us)
Async XLA Ops:
  6.5 518.2 %copy-start = (bf16[768,768]{1,0:T(8,128)(2,1)S(1)}, bf16[768,768]{1,0:T(8,128)(2,1)}, u32[]{:S(2)}) copy-start(bf16[768,768]{1,0:T(8,128)(2,1)} %param.11) | copy-start | bytes 3538948
  6.5 45.6 %all-gather.7.cloned.1.call-start = ((), (), s32[]{:S(2)}) async-start(), calls=%async_computation.3 | async-start | bytes 1769472 | tf_op jit(solution)/shard_map/all_gather | solution.py:74
  7.3 98.8 %all-gather.5.cloned.1.call-start = ((), (), s32[]{:S(2)}) async-start(), calls=%async_computation.2 | async-start | bytes 3342336 | tf_op jit(solution)/shard_map/all_gather | solution.py:79
  8.0 151.4 %all-gather.9.cloned.1.call-start = ((), (), s32[]{:S(2)}) async-start(), calls=%async_computation.4 | async-start | bytes 3342336 | tf_op jit(solution)/shard_map/all_gather | solution.py:80
  8.7 467.9 %reduce-scatter.5.cloned.1.call-start = ((), (), s32[]{:S(2)}) async-start(), calls=%async_computation.6 | async-start | bytes 73728 | tf_op jit(solution)/shard_map/reduce_scatter | solution.py:63
  174.3 4.6 copy-start.1
  188.2 4.6 copy-start.1
  203.2 4.6 copy-start.1
  218.2 4.6 copy-start.1
  233.2 4.6 copy-start.1
  248.1 4.6 copy-start.1
  263.1 4.6 copy-start.1
  278.1 4.6 copy-start.1
  293.1 4.6 copy-start.1
  308.1 4.6 copy-start.1
  323.0 4.6 copy-start.1
  338.0 4.6 copy-start.1
  353.0 4.6 copy-start.1
  368.0 4.6 copy-start.1
  383.0 4.6 copy-start.1
  398.0 4.6 copy-start.1
  442.5 81.2 %reduce-scatter.3.cloned.1.call-start = ((), (), s32[]{:S(2)}) async-start(), calls=%async_computation.5 | async-start | bytes 3538944 | tf_op jit(solution)/shard_map/reduce_scatter | solution.py:64
Sparse Core Ops, SparseCore 0:
  9.0 43.0 all-gather.6
  54.5 51.5 all-gather.4
  108.5 50.8 all-gather.8
  442.6 33.9 reduce-scatter.4
  479.0 44.6 reduce-scatter.2
where the time goes:
time: 534 us; the launch traced here: 532 us
  waiting for transfers between devices  191 us (36%)
  matrix products  166 us (31%)
  other arithmetic  77.2 us (14%)
  blocking collectives  58.7 us (11%)
  local copies, waits for them, and re-layouts  25.7 us (5%)
  between operations  13.2 us (2%)
    dot_general x16, matrix products, one_block(): jnp.einsum('hqk,khd->hqd', chances, value_heads, preferred_element_type=j...  87.4 us
    dot_general x16, matrix products, one_block(): jnp.einsum('qhd,khd->hqk', query_heads, key_heads, preferred_element_type...  77.1 us
    reduce_sum x16, other arithmetic, one_block(): jnp.sum(chances, axis=-1, dtype=jnp.float32)  69 us
    all_gather x1, waiting for transfers between devices, on_device(): lax.all_gather(keys, 'inner', axis=0, tiled=True)  52.2 us
    reduce_scatter x1, waiting for transfers between devices, combine_loop(): lax.psum_scatter(weighted * shrink[..., None], 'blk', scatter_dimension=1...  46.4 us
    all_gather x1, waiting for transfers between devices, on_device(): lax.all_gather(values, 'inner', axis=0, tiled=True)  43.1 us
    pmax x1, blocking collectives, combine_loop(): top = lax.pmax(run_max, 'blk')  33.8 us
    reduce_scatter x1, waiting for transfers between devices, combine_loop(): lax.psum_scatter(row_total * shrink, 'blk', scatter_dimension=1, tiled=True)  29.9 us
  transfers between devices with their start and end apart: 5, of which 5 were waited for; matrix products, arithmetic and copies ran while one was open for 3% of the time, Pallas kernels for 0%

commit v1 on v0

--- a/solution.py
+++ b/solution.py
@@ -76,7 +76,9 @@
     state_end = attend(
         starting,
         (
-            lax.all_gather(keys, "inner", axis=0, tiled=True),
+            jnp.concatenate(
+                lax.all_to_all(jnp.stack([keys] * lax.axis_size("inner")), "inner", 0, 0), axis=0
+            ),
             lax.all_gather(values, "inner", axis=0, tiled=True),
             lax.all_gather(flags, "inner", axis=0, tiled=True),
         ),

time: 534 us -> 490 us (0.918)
  waiting for transfers between devices: 191 us -> 105 us
  blocking collectives: 58.7 us -> 101 us
  starting transfers between devices: 0.16 us -> 8.1 us
  local copies, waits for them, and re-layouts: 25.7 us -> 18.9 us
    all_gather x1 -> x0, waiting for transfers between devices: 52.2 us -> none  [on_device(): lax.all_gather(keys, 'inner', axis=0, tiled=True)]
    all_gather x1, blocking collectives: 25 us -> 67.4 us  [on_device(): lax.all_gather(flags, 'inner', axis=0, tiled=True)]
    all_gather x1, waiting for transfers between devices: 17.7 us -> 0.01 us  [on_device(): query_all = lax.all_gather(queries, 'blk', axis=0, tiled=True)]
    all_gather x1, waiting for transfers between devices: 43.1 us -> 27.5 us  [on_device(): lax.all_gather(values, 'inner', axis=0, tiled=True)]
    all_to_all x0 -> x1, starting transfers between devices: none -> 7.98 us  [on_device(): lax.all_to_all(jnp.stack([keys] * lax.axis_size('inner')), 'inner', 0, 0)]
    unnamed x7 -> x8, local copies, waits for them, and re-layouts: 10.9 us -> 6.5 us
  transfers between devices with their start and end apart: 5 -> 5, of which waited for: 5 -> 3; matrix products, arithmetic and copies ran while one was open for 3% -> 4% of each run, Pallas kernels for 0% -> 0%
where the time goes in v1:
time: 490 us; the launch traced here: 489 us
  matrix products  166 us (34%)
  waiting for transfers between devices  105 us (21%)
  blocking collectives  101 us (21%)
  other arithmetic  76.5 us (16%)
  local copies, waits for them, and re-layouts  18.9 us (4%)
  between operations  13.2 us (3%)
  starting transfers between devices  8.1 us (2%)
    dot_general x16, matrix products, one_block(): jnp.einsum('hqk,khd->hqd', chances, value_heads, preferred_element_type=j...  87.4 us
    dot_general x16, matrix products, one_block(): jnp.einsum('qhd,khd->hqk', query_heads, key_heads, preferred_element_type...  77.1 us
    reduce_sum x16, other arithmetic, one_block(): jnp.sum(chances, axis=-1, dtype=jnp.float32)  69 us
    all_gather x1, blocking collectives, on_device(): lax.all_gather(flags, 'inner', axis=0, tiled=True)  67.4 us
    reduce_scatter x1, waiting for transfers between devices, combine_loop(): lax.psum_scatter(weighted * shrink[..., None], 'blk', scatter_dimension=1...  46.5 us
    pmax x1, blocking collectives, combine_loop(): top = lax.pmax(run_max, 'blk')  33.8 us
    reduce_scatter x1, waiting for transfers between devices, combine_loop(): lax.psum_scatter(row_total * shrink, 'blk', scatter_dimension=1, tiled=True)  29.9 us
    all_gather x1, waiting for transfers between devices, on_device(): lax.all_gather(values, 'inner', axis=0, tiled=True)  27.5 us
  transfers between devices with their start and end apart: 5, of which 3 were waited for; matrix products, arithmetic and copies ran while one was open for 4% of the time, Pallas kernels for 0%

profile of v1, /device:TPU:0, one launch (start us, length us, event | category | flops | bytes accessed | tf_op | source)
XLA Modules:
  0.0 489.2 jit_solution(9422314213067358289)
XLA Ops:
  11.4 8.0 %all-to-all-start = ((bf16[16,128,768]{1,2,0:T(8,128)(2,1)}), bf16[16,128,768]{1,2,0:T(8,128)(2,1)}, u32[]{:S(2)}, u32[]{:S(2)}) async-start(bf16[16,128,768]{1,2,0:T(8,128)(2,1)} %stack.2), calls=%async_computation | async-start | bytes 6291456 | tf_op jit(solution)/shard_map/all_to_all | solution.py:80
  19.4 67.4 %all-gather = bf16[16,1,128]{2,1,0:T(2,128)(2,1)S(1)} all-gather(bf16[1,1,128]{2,1,0:T(2,128)(2,1)S(1)} %convert_bitcast_fusion), channel_id=1, replica_groups=mesh['blk'=8,'inner'=16] {'inner'}, dimensions={0}, use_global_device_ids=true | all-gather | bytes 4352 | tf_op jit(solution)/shard_map/all_gather | solution.py:83
  88.6 27.5 %all-gather.6.cloned.1.call-done = bf16[2048,768]{1,0:T(8,128)(2,1)} async-done(((bf16[128,768]{1,0:T(8,128)(2,1)}), bf16[2048,768]{1,0:T(8,128)(2,1)}) %all-gather.6.cloned.1.call-update) | async-done | bytes 3145744 | tf_op jit(solution)/shard_map/all_gather | solution.py:82
  126.2 238.6 %while.15 = (s32[]{:T(128)}, f32[12,1024]{1,0:T(8,128)S(1)}, f32[12,1024]{1,0:T(8,128)S(1)}, f32[12,1024,64]{1,2,0:T(8,128)}, bf16[16,128]{1,0:T(8,128)(2,1)S(1)...) while((s32[]{:T(128)}, f32[12,1024]{1,0:T(8,128)S(1)}, ...), condition=%wide.region_3.4_spmd.clone, body=%wide.region_0.3_spmd.clone.sunk | while | flops 425521536 | bytes 53086096 | solution.py:43
  140.2 4.8 bitcast_reduce_fusion.2
  149.6 5.5 %fusion.25 = f32[12,1024,64]{1,2,0:T(8,128)} fusion(f32[12,1024,64]{1,2,0:T(8,128)} %get-tuple-element.187, f32[12,1024]{1,0:T(8,128)S(1)} %get-tuple-element.173, pred[]{:T(512)S(6)} %compare.3, bf16[16,128,12,64]{1,3,2,0:T(8,128)(2,1)} %get-tuple-element.201, s32[]{:T(128)} %get-tuple-element.184, f32[12,128,1024]{2,1,0:T(8,128)S(1)} %copy-done.1, ...), kind=kOutput, calls=%fused_computation.7.clone.1 | convolution fusion | flops 209977344 | bytes 12878465 | tf_op jit(solution)/shard_map/while/body/eval_jaxpr/hqk,khd->hqd/dot_general | solution.py:38
  155.1 4.8 bitcast_reduce_fusion.2
  164.6 5.5 %fusion.25 = f32[12,1024,64]{1,2,0:T(8,128)} fusion(f32[12,1024,64]{1,2,0:T(8,128)} %get-tuple-element.187, f32[12,1024]{1,0:T(8,128)S(1)} %get-tuple-element.173, pred[]{:T(512)S(6)} %compare.3, bf16[16,128,12,64]{1,3,2,0:T(8,128)(2,1)} %get-tuple-element.201, s32[]{:T(128)} %get-tuple-element.184, f32[12,128,1024]{2,1,0:T(8,128)S(1)} %copy-done.1, ...), kind=kOutput, calls=%fused_computation.7.clone.1 | convolution fusion | flops 209977344 | bytes 12878465 | tf_op jit(solution)/shard_map/while/body/eval_jaxpr/hqk,khd->hqd/dot_general | solution.py:38
  179.6 5.5 %fusion.25 = f32[12,1024,64]{1,2,0:T(8,128)} fusion(f32[12,1024,64]{1,2,0:T(8,128)} %get-tuple-element.187, f32[12,1024]{1,0:T(8,128)S(1)} %get-tuple-element.173, pred[]{:T(512)S(6)} %compare.3, bf16[16,128,12,64]{1,3,2,0:T(8,128)(2,1)} %get-tuple-element.201, s32[]{:T(128)} %get-tuple-element.184, f32[12,128,1024]{2,1,0:T(8,128)S(1)} %copy-done.1, ...), kind=kOutput, calls=%fused_computation.7.clone.1 | convolution fusion | flops 209977344 | bytes 12878465 | tf_op jit(solution)/shard_map/while/body/eval_jaxpr/hqk,khd->hqd/dot_general | solution.py:38
  194.5 5.5 %fusion.25 = f32[12,1024,64]{1,2,0:T(8,128)} fusion(f32[12,1024,64]{1,2,0:T(8,128)} %get-tuple-element.187, f32[12,1024]{1,0:T(8,128)S(1)} %get-tuple-element.173, pred[]{:T(512)S(6)} %compare.3, bf16[16,128,12,64]{1,3,2,0:T(8,128)(2,1)} %get-tuple-element.201, s32[]{:T(128)} %get-tuple-element.184, f32[12,128,1024]{2,1,0:T(8,128)S(1)} %copy-done.1, ...), kind=kOutput, calls=%fused_computation.7.clone.1 | convolution fusion | flops 209977344 | bytes 12878465 | tf_op jit(solution)/shard_map/while/body/eval_jaxpr/hqk,khd->hqd/dot_general | solution.py:38
  209.5 5.5 %fusion.25 = f32[12,1024,64]{1,2,0:T(8,128)} fusion(f32[12,1024,64]{1,2,0:T(8,128)} %get-tuple-element.187, f32[12,1024]{1,0:T(8,128)S(1)} %get-tuple-element.173, pred[]{:T(512)S(6)} %compare.3, bf16[16,128,12,64]{1,3,2,0:T(8,128)(2,1)} %get-tuple-element.201, s32[]{:T(128)} %get-tuple-element.184, f32[12,128,1024]{2,1,0:T(8,128)S(1)} %copy-done.1, ...), kind=kOutput, calls=%fused_computation.7.clone.1 | convolution fusion | flops 209977344 | bytes 12878465 | tf_op jit(solution)/shard_map/while/body/eval_jaxpr/hqk,khd->hqd/dot_general | solution.py:38
  224.5 5.5 %fusion.25 = f32[12,1024,64]{1,2,0:T(8,128)} fusion(f32[12,1024,64]{1,2,0:T(8,128)} %get-tuple-element.187, f32[12,1024]{1,0:T(8,128)S(1)} %get-tuple-element.173, pred[]{:T(512)S(6)} %compare.3, bf16[16,128,12,64]{1,3,2,0:T(8,128)(2,1)} %get-tuple-element.201, s32[]{:T(128)} %get-tuple-element.184, f32[12,128,1024]{2,1,0:T(8,128)S(1)} %copy-done.1, ...), kind=kOutput, calls=%fused_computation.7.clone.1 | convolution fusion | flops 209977344 | bytes 12878465 | tf_op jit(solution)/shard_map/while/body/eval_jaxpr/hqk,khd->hqd/dot_general | solution.py:38
  239.5 5.5 %fusion.25 = f32[12,1024,64]{1,2,0:T(8,128)} fusion(f32[12,1024,64]{1,2,0:T(8,128)} %get-tuple-element.187, f32[12,1024]{1,0:T(8,128)S(1)} %get-tuple-element.173, pred[]{:T(512)S(6)} %compare.3, bf16[16,128,12,64]{1,3,2,0:T(8,128)(2,1)} %get-tuple-element.201, s32[]{:T(128)} %get-tuple-element.184, f32[12,128,1024]{2,1,0:T(8,128)S(1)} %copy-done.1, ...), kind=kOutput, calls=%fused_computation.7.clone.1 | convolution fusion | flops 209977344 | bytes 12878465 | tf_op jit(solution)/shard_map/while/body/eval_jaxpr/hqk,khd->hqd/dot_general | solution.py:38
  254.5 5.5 %fusion.25 = f32[12,1024,64]{1,2,0:T(8,128)} fusion(f32[12,1024,64]{1,2,0:T(8,128)} %get-tuple-element.187, f32[12,1024]{1,0:T(8,128)S(1)} %get-tuple-element.173, pred[]{:T(512)S(6)} %compare.3, bf16[16,128,12,64]{1,3,2,0:T(8,128)(2,1)} %get-tuple-element.201, s32[]{:T(128)} %get-tuple-element.184, f32[12,128,1024]{2,1,0:T(8,128)S(1)} %copy-done.1, ...), kind=kOutput, calls=%fused_computation.7.clone.1 | convolution fusion | flops 209977344 | bytes 12878465 | tf_op jit(solution)/shard_map/while/body/eval_jaxpr/hqk,khd->hqd/dot_general | solution.py:38
  269.4 5.5 %fusion.25 = f32[12,1024,64]{1,2,0:T(8,128)} fusion(f32[12,1024,64]{1,2,0:T(8,128)} %get-tuple-element.187, f32[12,1024]{1,0:T(8,128)S(1)} %get-tuple-element.173, pred[]{:T(512)S(6)} %compare.3, bf16[16,128,12,64]{1,3,2,0:T(8,128)(2,1)} %get-tuple-element.201, s32[]{:T(128)} %get-tuple-element.184, f32[12,128,1024]{2,1,0:T(8,128)S(1)} %copy-done.1, ...), kind=kOutput, calls=%fused_computation.7.clone.1 | convolution fusion | flops 209977344 | bytes 12878465 | tf_op jit(solution)/shard_map/while/body/eval_jaxpr/hqk,khd->hqd/dot_general | solution.py:38
  284.4 5.5 %fusion.25 = f32[12,1024,64]{1,2,0:T(8,128)} fusion(f32[12,1024,64]{1,2,0:T(8,128)} %get-tuple-element.187, f32[12,1024]{1,0:T(8,128)S(1)} %get-tuple-element.173, pred[]{:T(512)S(6)} %compare.3, bf16[16,128,12,64]{1,3,2,0:T(8,128)(2,1)} %get-tuple-element.201, s32[]{:T(128)} %get-tuple-element.184, f32[12,128,1024]{2,1,0:T(8,128)S(1)} %copy-done.1, ...), kind=kOutput, calls=%fused_computation.7.clone.1 | convolution fusion | flops 209977344 | bytes 12878465 | tf_op jit(solution)/shard_map/while/body/eval_jaxpr/hqk,khd->hqd/dot_general | solution.py:38
  299.4 5.5 %fusion.25 = f32[12,1024,64]{1,2,0:T(8,128)} fusion(f32[12,1024,64]{1,2,0:T(8,128)} %get-tuple-element.187, f32[12,1024]{1,0:T(8,128)S(1)} %get-tuple-element.173, pred[]{:T(512)S(6)} %compare.3, bf16[16,128,12,64]{1,3,2,0:T(8,128)(2,1)} %get-tuple-element.201, s32[]{:T(128)} %get-tuple-element.184, f32[12,128,1024]{2,1,0:T(8,128)S(1)} %copy-done.1, ...), kind=kOutput, calls=%fused_computation.7.clone.1 | convolution fusion | flops 209977344 | bytes 12878465 | tf_op jit(solution)/shard_map/while/body/eval_jaxpr/hqk,khd->hqd/dot_general | solution.py:38
  314.4 5.5 %fusion.25 = f32[12,1024,64]{1,2,0:T(8,128)} fusion(f32[12,1024,64]{1,2,0:T(8,128)} %get-tuple-element.187, f32[12,1024]{1,0:T(8,128)S(1)} %get-tuple-element.173, pred[]{:T(512)S(6)} %compare.3, bf16[16,128,12,64]{1,3,2,0:T(8,128)(2,1)} %get-tuple-element.201, s32[]{:T(128)} %get-tuple-element.184, f32[12,128,1024]{2,1,0:T(8,128)S(1)} %copy-done.1, ...), kind=kOutput, calls=%fused_computation.7.clone.1 | convolution fusion | flops 209977344 | bytes 12878465 | tf_op jit(solution)/shard_map/while/body/eval_jaxpr/hqk,khd->hqd/dot_general | solution.py:38
  329.4 5.5 %fusion.25 = f32[12,1024,64]{1,2,0:T(8,128)} fusion(f32[12,1024,64]{1,2,0:T(8,128)} %get-tuple-element.187, f32[12,1024]{1,0:T(8,128)S(1)} %get-tuple-element.173, pred[]{:T(512)S(6)} %compare.3, bf16[16,128,12,64]{1,3,2,0:T(8,128)(2,1)} %get-tuple-element.201, s32[]{:T(128)} %get-tuple-element.184, f32[12,128,1024]{2,1,0:T(8,128)S(1)} %copy-done.1, ...), kind=kOutput, calls=%fused_computation.7.clone.1 | convolution fusion | flops 209977344 | bytes 12878465 | tf_op jit(solution)/shard_map/while/body/eval_jaxpr/hqk,khd->hqd/dot_general | solution.py:38
  344.3 5.5 %fusion.25 = f32[12,1024,64]{1,2,0:T(8,128)} fusion(f32[12,1024,64]{1,2,0:T(8,128)} %get-tuple-element.187, f32[12,1024]{1,0:T(8,128)S(1)} %get-tuple-element.173, pred[]{:T(512)S(6)} %compare.3, bf16[16,128,12,64]{1,3,2,0:T(8,128)(2,1)} %get-tuple-element.201, s32[]{:T(128)} %get-tuple-element.184, f32[12,128,1024]{2,1,0:T(8,128)S(1)} %copy-done.1, ...), kind=kOutput, calls=%fused_computation.7.clone.1 | convolution fusion | flops 209977344 | bytes 12878465 | tf_op jit(solution)/shard_map/while/body/eval_jaxpr/hqk,khd->hqd/dot_general | solution.py:38
  359.3 5.5 %fusion.25 = f32[12,1024,64]{1,2,0:T(8,128)} fusion(f32[12,1024,64]{1,2,0:T(8,128)} %get-tuple-element.187, f32[12,1024]{1,0:T(8,128)S(1)} %get-tuple-element.173, pred[]{:T(512)S(6)} %compare.3, bf16[16,128,12,64]{1,3,2,0:T(8,128)(2,1)} %get-tuple-element.201, s32[]{:T(128)} %get-tuple-element.184, f32[12,128,1024]{2,1,0:T(8,128)S(1)} %copy-done.1, ...), kind=kOutput, calls=%fused_computation.7.clone.1 | convolution fusion | flops 209977344 | bytes 12878465 | tf_op jit(solution)/shard_map/while/body/eval_jaxpr/hqk,khd->hqd/dot_general | solution.py:38
  364.9 33.8 %pmax.7 = f32[12,1024]{1,0:T(8,128)S(1)} all-reduce(f32[12,1024]{1,0:T(8,128)S(1)} %get-tuple-element.50), channel_id=1, replica_groups=mesh['blk'=8,'inner'=16] {'blk'}, use_global_device_ids=true, to_apply=%region_4.5 | all-reduce | flops 12288 | bytes 98304 | tf_op jit(solution)/shard_map/pmax | solution.py:60
  403.5 29.9 %reduce-scatter.5.cloned.1.call-done = f32[12,128]{1,0:T(8,128)} async-done(((f32[12,1024]{1,0:T(8,128)}), f32[12,128]{1,0:T(8,128)}) %reduce-scatter.5.cloned.1.call-update) | async-done | bytes 6160 | tf_op jit(solution)/shard_map/reduce_scatter | solution.py:63
  434.1 46.5 %reduce-scatter.3.cloned.1.call-done = f32[12,128,64]{1,2,0:T(8,128)} async-done(((f32[12,1024,64]{1,2,0:T(8,128)}), f32[12,128,64]{1,2,0:T(8,128)}) %reduce-scatter.3.cloned.1.call-update) | async-done | bytes 393232 | tf_op jit(solution)/shard_map/reduce_scatter | solution.py:64
  (157 shorter events, 170.0 us)
Async XLA Ops:
  6.5 475.1 %copy-start = (bf16[768,768]{1,0:T(8,128)(2,1)S(1)}, bf16[768,768]{1,0:T(8,128)(2,1)}, u32[]{:S(2)}) copy-start(bf16[768,768]{1,0:T(8,128)(2,1)} %param.11) | copy-start | bytes 3538948
  6.5 80.4 %all-gather.4.cloned.1.call-start = ((), (), s32[]{:S(2)}) async-start(), calls=%async_computation.3 | async-start | bytes 1769472 | tf_op jit(solution)/shard_map/all_gather | solution.py:74
  7.3 108.9 %all-gather.6.cloned.1.call-start = ((), (), s32[]{:S(2)}) async-start(), calls=%async_computation.4 | async-start | bytes 3342336 | tf_op jit(solution)/shard_map/all_gather | solution.py:82
  11.4 8.1 %copy-start.2 = (s32[128]{0:T(128)S(1)}, s32[128]{0:T(128)}, u32[]{:S(2)}) copy-start(s32[128]{0:T(128)} %param.10) | copy-start | bytes 1540
  11.4 114.9 %all-to-all-start = ((bf16[16,128,768]{1,2,0:T(8,128)(2,1)}), bf16[16,128,768]{1,2,0:T(8,128)(2,1)}, u32[]{:S(2)}, u32[]{:S(2)}) async-start(bf16[16,128,768]{1,2,0:T(8,128)(2,1)} %stack.2), calls=%async_computation | async-start | bytes 6291456 | tf_op jit(solution)/shard_map/all_to_all | solution.py:80
  19.3 414.0 %reduce-scatter.5.cloned.1.call-start = ((), (), s32[]{:S(2)}) async-start(), calls=%async_computation.6 | async-start | bytes 73728 | tf_op jit(solution)/shard_map/reduce_scatter | solution.py:63
  131.1 4.6 copy-start.1
  145.0 4.6 copy-start.1
  160.0 4.6 copy-start.1
  175.0 4.6 copy-start.1
  189.9 4.6 copy-start.1
  204.9 4.6 copy-start.1
  219.9 4.6 copy-start.1
  234.9 4.6 copy-start.1
  249.9 4.6 copy-start.1
  264.8 4.6 copy-start.1
  279.8 4.6 copy-start.1
  294.8 4.6 copy-start.1
  309.8 4.6 copy-start.1
  324.8 4.6 copy-start.1
  339.7 4.6 copy-start.1
  354.7 4.6 copy-start.1
  399.3 81.3 %reduce-scatter.3.cloned.1.call-start = ((), (), s32[]{:S(2)}) async-start(), calls=%async_computation.5 | async-start | bytes 3538944 | tf_op jit(solution)/shard_map/reduce_scatter | solution.py:64
Sparse Core Ops, SparseCore 0:
  9.0 50.5 all-gather.3
  62.0 54.0 all-gather.5
  399.4 33.9 reduce-scatter.4
  435.8 44.7 reduce-scatter.2
